TPU v7x, 32 devices: a whole 2x2x4 slice. The times are simulated.
32 devices in a mesh: group: 2 (over x), tile: 16 (over z, y, core).
Axes of the slice: x: 2, y: 2, z: 4, core: 2. Of those that a mesh axis runs over, the one named last changes fastest.
Arguments:
- latents: bfloat16 [384, 16, 128], P(('group', 'tile')), parts along dimension 0, may hold values from -6 to 6
- clip_index: int32 [8], P('group'), parts along dimension 0, may hold values from 0 to 1, never falling along the last dimension, each value on 1 to 3 neighbouring positions
- first_conv: bfloat16 [3, 3, 3, 16, 384], replicated, may hold values from -0.3125 to 0.3125
- first_gain: float32 [384], replicated, may hold values from 0.4 to 1.6
- middle_conv: bfloat16 [3, 3, 3, 384, 384], replicated, may hold values from -0.0625 to 0.0625
- head_gain: float32 [384], replicated, may hold values from 0.4 to 1.6
- head_weight: bfloat16 [384, 48], replicated, may hold values from -0.3125 to 0.3125
Outputs:
- pixels: float32 [32, 2, 3, 48, 128], P(('group', 'tile')), parts along dimension 0
There are 2 independent parts, one for each index of `group`. A program takes and returns all parts, laid end to end along the dimension named above; an argument that names none is the same for every part. Nothing has to cross between parts.
Inputs may be any that keep to these rules, and one draw needn't show every extreme that they name: `clip_index`: clip numbers never fall along the frames; each clip holds 1 to 3 consecutive frames.
All inputs are finite; a program needn't handle non-finite values.
Results may differ from a plain program's by a relative error of at most 0.01.
Values may be sent and summed in bfloat16 or wider, within the bound.
A program may use at most 128 MiB of HBM per device.

v0:
```python
import functools

import jax
import jax.numpy as jnp
from jax import lax
from jax.experimental import pallas as pl
from jax.experimental.pallas import tpu as pltpu
from jax.sharding import PartitionSpec as P

WS = 16
TF = 2
LANES = 128
GAP = LANES // 2
WIDE = WS + 5
HALF = (WIDE + 1) // 2


def norm_act(x, gain):
    scale = lax.rsqrt(jnp.mean(x * x, axis=-1, keepdims=True) + 1e-06)
    h = x * scale * (0.5 * gain)
    return h + h * jnp.tanh(h)


def row_shift(x, by):
    rows = lax.broadcasted_iota(jnp.int32, x.shape, 0)
    n = x.shape[0]
    if by > 0:
        return jnp.where(rows == 0, 0.0, pltpu.roll(x, 1, 0))
    return jnp.where(rows == n - 1, 0.0, pltpu.roll(x, n - 1, 0))


def exchange_kernel(sizes, lat_ref, got, pad_a, pad_b, packed, stage, send_sem, recv_sem, own_sem):
    tiles, strips, frames, shard_rows = sizes
    quarters = tiles // frames
    blocks = tiles // strips
    offset = strips // 2 - 1
    me = lax.axis_index("tile")
    barrier = pltpu.get_barrier_semaphore()
    for step in range(1, tiles):
        pl.semaphore_signal(barrier, inc=1, device_id={"tile": lax.rem(me + step, tiles)})

    wl = lat_ref.shape[1]
    values = lat_ref[...].astype(jnp.float32)
    spare = jnp.zeros((2 * LANES - values.shape[0], wl), jnp.float32)
    for pad, rows in ((pad_a, values[:LANES]), (pad_b, jnp.concatenate([values[LANES:], spare]))):
        pad[:8] = jnp.zeros((8, LANES), jnp.float32)
        pad[8 + wl :] = jnp.zeros((WS, LANES), jnp.float32)
        pad[8 : 8 + wl] = rows.T
    low = lax.broadcasted_iota(jnp.int32, (HALF, LANES), 1) < LANES // 2
    for s in range(strips):
        at = WS * s + 8 - 3
        packed[s, :WIDE] = pad_a[at : at + WIDE]
        upper = pltpu.roll(pad_b[at + HALF : at + 2 * HALF], LANES // 2, 1)
        packed[s, WIDE:] = jnp.where(low, pad_b[at : at + HALF], upper)
        stage[s] = packed[s].astype(jnp.bfloat16)
    pl.semaphore_wait(barrier, tiles - 1)

    frame = me // quarters
    quarter = me % quarters

    def each_send(act):
        for ahead in range(3):
            block = frame // TF + ahead
            slot = (2 * TF - TF * ahead + frame % TF) * quarters + quarter

            @pl.when(block < blocks)
            def _():
                @pl.loop(0, strips)
                def _(j):
                    s = (j + me) % strips
                    to = (block * strips + s + offset) % tiles

                    @pl.when(to != me)
                    def _():
                        act(
                            pltpu.make_async_remote_copy(
                                src_ref=stage.at[s],
                                dst_ref=got.at[slot],
                                send_sem=send_sem.at[ahead * strips + s],
                                recv_sem=recv_sem.at[slot],
                                device_id={"tile": to},
                            ),
                            None,
                        )

                    @pl.when(to == me)
                    def _():
                        act(None, pltpu.make_async_copy(stage.at[s], got.at[slot], own_sem))

    def start(remote, local):
        (remote if local is None else local).start()

    def finish(remote, local):
        if local is None:
            remote.wait_send()
        else:
            local.wait()

    each_send(start)
    mine = (me + tiles - offset) % tiles // strips

    @pl.loop(0, 3 * TF * quarters)
    def _(slot):
        source = (TF * mine - 2 * TF) * quarters + slot

        @pl.when(jnp.logical_and(source >= 0, source != me))
        def _():
            pltpu.make_async_remote_copy(
                src_ref=stage.at[0],
                dst_ref=got.at[slot],
                send_sem=send_sem.at[0],
                recv_sem=recv_sem.at[slot],
                device_id={"tile": me},
            ).wait_recv()

    each_send(finish)


def decode_kernel(
    sizes, clip, got_ref, w1_ref, g1_ref, wm_hbm, g2_ref, hw_ref, out_ref,
    wm, act, firstb, fscr, acc, outw, w1, main, tail, rowtap, z_ref, sem,
):
    tiles, strips, hl, clat, shard_rows = sizes
    ch = g1_ref.shape[-1]
    patch = hw_ref.shape[0] // 3
    half = patch // 2
    aw = WS + 3
    ow = WS + 1
    lanes = WS * half
    rotated = (lax.axis_index("tile") + tiles - (strips // 2 - 1)) % tiles
    strip = rotated % strips
    block = rotated // strips
    scal = []
    for i in range(3 * TF):
        at = block * TF - 2 * TF + i
        scal.append(jnp.where(at < 0, -1, clip[jnp.maximum(at, 0)]))
    g1 = g1_ref[...].reshape(1, ch)
    g2 = g2_ref[...].reshape(1, ch)

    def tap_copies(dt):
        return [
            pltpu.make_async_copy(
                wm_hbm.at[dt, dr, dc],
                wm.at[pl.ds(dc * ch, ch), pl.ds((3 * dt + dr) * ch, ch)],
                sem.at[dt],
            )
            for dr in range(3)
            for dc in range(3)
        ]

    for dt in (2, 1, 0):
        for copy in tap_copies(dt):
            copy.start()

    group = 3 * clat
    w1[...] = jnp.zeros_like(w1)
    for dt in range(3):
        for dr in range(3):
            w1[dt, dr * GAP : dr * GAP + group] = w1_ref[dt, dr * group : (dr + 1) * group]
    wide = rowtap.shape[0] // (hl + 2)
    rowtap[:wide] = jnp.zeros((wide, LANES), jnp.float32)
    rowtap[(hl + 1) * wide :] = jnp.zeros((wide, LANES), jnp.float32)
    at_lane = lax.broadcasted_iota(jnp.int32, (wide, LANES), 1)
    quarters = hl // shard_rows
    per = LANES // clat

    for f in range(3 * TF):

        @pl.when(block * TF - 2 * TF + f < 0)
        def _(f=f):
            z_ref[f] = jnp.zeros(z_ref.shape[1:], jnp.bfloat16)

        @pl.when(block * TF - 2 * TF + f >= 0)
        def _(f=f):
            for q in range(quarters):
                main[q] = got_ref[f * quarters + q].astype(jnp.float32)
                tail[q, :HALF] = main[q, WIDE:]
                tail[q, HALF : 2 * HALF] = pltpu.roll(main[q, WIDE:], LANES // 2, 1)
                for first_row, count, x in ((0, per, main.at[q]), (per, shard_rows - per, tail.at[q])):
                    shifts = [x[dc : dc + wide] for dc in range(3)]
                    for r in range(count):
                        y = jnp.zeros((wide, LANES), jnp.float32)
                        for dc in (2, 1, 0):
                            turn = (dc - r) * clat % LANES
                            moved = pltpu.roll(shifts[dc], turn, 1) if turn else shifts[dc]
                            y = jnp.where(at_lane < (dc + 1) * clat, moved, y)
                        start = (1 + q * shard_rows + first_row + r) * wide
                        rowtap[start : start + wide] = y

            for w in range(aw):
                v = [
                    rowtap[pl.ds(dr * wide + w, hl, stride=wide), :] for dr in range(3)
                ]
                low = v[0] + pltpu.roll(v[1], GAP, 1)
                z_ref[f, w, :, :LANES] = low.astype(jnp.bfloat16)
                z_ref[f, w, :, LANES:] = v[2].astype(jnp.bfloat16)

    for f in range(TF + 2):
        if f == 0:
            needed = scal[2] == scal[4]
        elif f == 1:
            needed = jnp.logical_or(scal[3] == scal[4], scal[3] == scal[5])
        else:
            needed = scal[4] == scal[4]

        @pl.when(needed)
        def _(f=f):
            taps = []
            for dt in range(3):
                keep = (scal[f + dt] == scal[f + 2]).astype(jnp.float32)
                lhs = z_ref[f + dt].reshape(aw * hl, z_ref.shape[-1])
                taps.append(lhs * keep.astype(jnp.bfloat16) if dt < 2 else lhs)
            fscr[...] = jnp.dot(
                jnp.concatenate(taps, axis=-1), w1[...].reshape(-1, ch),
                preferred_element_type=jnp.float32,
            ).reshape(aw, hl, ch)

            for w in range(aw):
                rounded = fscr[w].astype(jnp.bfloat16)
                if f >= 2:
                    firstb[f - 2, w] = rounded
                value = norm_act(rounded.astype(jnp.float32), g1)
                if w < 2:
                    value = value * (strip > 0).astype(jnp.float32)
                if w == aw - 1:
                    value = value * (strip < strips - 1).astype(jnp.float32)
                act[f, w] = value.astype(jnp.bfloat16)

    wide_out = 3 * ch

    def unit(f, start, count):
        lhs = jnp.concatenate(
            [act[f, pl.ds(dc, ow)].reshape(ow * hl, ch) for dc in range(3)], axis=-1
        )
        taps = wm[:, start * wide_out : (start + count) * wide_out]
        return jnp.dot(lhs, taps, preferred_element_type=jnp.float32)

    def arrived(dt):
        for copy in tap_copies(dt):
            copy.wait()

    arrived(2)
    acc[:, :wide_out] = unit(3, 2, 1)
    arrived(1)

    @pl.when(scal[4] == scal[5])
    def _():
        both = unit(2, 1, 2)
        acc[:, :wide_out] += both[:, :wide_out]
        acc[:, wide_out:] = both[:, wide_out:]

    @pl.when(scal[4] != scal[5])
    def _():
        acc[:, wide_out:] = unit(2, 2, 1)

    arrived(0)

    @pl.when(scal[3] == scal[5])
    def _():
        acc[...] += unit(1, 0, 2)

    @pl.when(jnp.logical_and(scal[3] == scal[4], scal[3] != scal[5]))
    def _():
        acc[:, wide_out:] += unit(1, 1, 1)

    @pl.when(scal[2] == scal[4])
    def _():
        acc[:, wide_out:] += unit(0, 0, 1)

    rows = lax.broadcasted_iota(jnp.int32, (3 * patch, 6 * lanes), 0)
    cols = lax.broadcasted_iota(jnp.int32, (3 * patch, 6 * lanes), 1)
    odd = cols // (3 * lanes)
    colour = (cols // lanes) % 3
    want = colour * patch + (cols % lanes + half * odd) % patch
    spread = (rows == want).astype(jnp.bfloat16)
    head = lax.dot_general(
        hw_ref[...], spread, (((0,), (0,)), ((), ())), preferred_element_type=jnp.float32
    ).astype(jnp.bfloat16)
    lane = lax.broadcasted_iota(jnp.int32, (hl, lanes), 1)

    for fo in range(TF):
        for w in range(ow):
            part = acc[w * hl : (w + 1) * hl, (1 - fo) * wide_out : (2 - fo) * wide_out]
            summed = (
                firstb[fo, w + 1].astype(jnp.float32)
                + row_shift(part[:, :ch], 1)
                + part[:, ch : 2 * ch]
                + row_shift(part[:, 2 * ch :], -1)
            )
            value = norm_act(summed, g2)
            if w == 0:
                value = value * (strip > 0).astype(jnp.float32)
            outw[fo, w % 2, w // 2] = value.astype(jnp.bfloat16)

        p_odd = jnp.dot(
            outw[fo, 0].reshape(-1, ch), head[:, 3 * lanes :], preferred_element_type=jnp.float32
        )
        p_even = jnp.dot(
            outw[fo, 1, : WS // 2].reshape(-1, ch), head[:, : 3 * lanes],
            preferred_element_type=jnp.float32,
        )
        for k in range(3):
            front = jnp.zeros((hl, lanes), jnp.float32)
            back = jnp.zeros((hl, lanes), jnp.float32)
            for i in range(WS // 2):
                piece = p_even[i * hl : (i + 1) * hl, k * lanes : (k + 1) * lanes]
                front = jnp.where(lane // patch == i, piece, front)
            for i in range(WS // 2 + 1):
                piece = p_odd[i * hl : (i + 1) * hl, k * lanes : (k + 1) * lanes]
                back = jnp.where((lane + half) // patch == i, piece, back)
            out_ref[fo, k] = front + back


def per_device(latents, clip_index, first_conv, first_gain, middle_conv, head_gain, head_weight):
    tiles = lax.axis_size("tile")
    shard_rows, clat, wl = latents.shape
    ch = first_gain.shape[0]
    frames = clip_index.shape[0]
    hl = tiles * shard_rows // frames
    strips = wl // WS
    half = head_weight.shape[1] // 6
    aw = WS + 3
    quarters = tiles // frames
    slots = 3 * TF * quarters
    got = pl.pallas_call(
        functools.partial(exchange_kernel, (tiles, strips, frames, shard_rows)),
        out_shape=jax.ShapeDtypeStruct((slots, WIDE + HALF, LANES), jnp.bfloat16),
        in_specs=[pl.BlockSpec(memory_space=pltpu.VMEM)],
        out_specs=pl.BlockSpec(memory_space=pl.ANY),
        scratch_shapes=[
            pltpu.VMEM((8 + wl + WS, LANES), jnp.float32),
            pltpu.VMEM((8 + wl + WS, LANES), jnp.float32),
            pltpu.VMEM((strips, WIDE + HALF, LANES), jnp.float32),
            pltpu.VMEM((strips, WIDE + HALF, LANES), jnp.bfloat16),
            pltpu.SemaphoreType.DMA((3 * strips,)),
            pltpu.SemaphoreType.DMA((slots,)),
            pltpu.SemaphoreType.DMA,
        ],
        compiler_params=pltpu.CompilerParams(collective_id=0, has_side_effects=True),
    )(latents.reshape(shard_rows * clat, wl))
    vm = pl.BlockSpec(memory_space=pltpu.VMEM)
    out = pl.pallas_call(
        functools.partial(decode_kernel, (tiles, strips, hl, clat, shard_rows)),
        out_shape=jax.ShapeDtypeStruct((TF, 3, hl, WS * half), jnp.float32),
        in_specs=[
            pl.BlockSpec(memory_space=pltpu.SMEM), vm, vm, vm,
            pl.BlockSpec(memory_space=pl.ANY), vm, vm,
        ],
        out_specs=vm,
        scratch_shapes=[
            pltpu.VMEM((3 * ch, 9 * ch), jnp.bfloat16),
            pltpu.VMEM((TF + 2, aw, hl, ch), jnp.bfloat16),
            pltpu.VMEM((TF, aw, hl, ch), jnp.bfloat16),
            pltpu.VMEM((aw, hl, ch), jnp.float32),
            pltpu.VMEM(((WS + 1) * hl, TF * 3 * ch), jnp.float32),
            pltpu.VMEM((TF, 2, WS // 2 + 1, hl, ch), jnp.bfloat16),
            pltpu.VMEM((3, 2 * LANES, ch), jnp.bfloat16),
            pltpu.VMEM((quarters, WIDE + HALF, LANES), jnp.float32),
            pltpu.VMEM((quarters, WIDE + HALF, LANES), jnp.float32),
            pltpu.VMEM(((hl + 2) * 24, LANES), jnp.float32),
            pltpu.VMEM((3 * TF, aw, hl, 2 * LANES), jnp.bfloat16),
            pltpu.SemaphoreType.DMA((3,)),
        ],
        compiler_params=pltpu.CompilerParams(vmem_limit_bytes=60 * 1024 * 1024),
    )(
        clip_index, got, first_conv.reshape(3, 9 * clat, ch), first_gain, middle_conv,
        head_gain, head_weight.T,
    )
    return out[None]


def solution(mesh):
    placed = (P(("group", "tile"), None, None), P("group"), P(), P(), P(), P(), P())
    return jax.shard_map(
        per_device,
        mesh=mesh,
        in_specs=placed,
        out_specs=P(("group", "tile"), None, None, None, None),
        check_vma=False,
    )
```

profile of v0, /device:TPU:0, one launch (start us, length us, event | category | flops | bytes accessed | tf_op | source)
XLA Modules:
  0.0 34.4 jit_solution(5785756171756786586)
XLA Ops:
  0.0 10.9 %shard_map.73.got_ref = bf16[24,32,128]{2,1,0:T(8,128)(2,1)} custom-call(bf16[192,128]{1,0:T(8,128)(2,1)} %bitcast.5), custom_call_target="tpu_custom_call" | custom-call | tf_op jit(solution)/shard_map/pallas_call | solution.py:325
  10.9 23.3 %shard_map.74 = f32[2,3,48,128]{3,2,1,0:T(8,128)} custom-call(s32[4]{0:T(128)} %clip.1, bf16[24,32,128]{2,1,0:T(8,128)(2,1)} %shard_map.73.got_ref, bf16[3,144,384]{2,1,0:T(8,128)(2,1)} %bitcast.4, f32[384]{0:T(512)} %g1_ref.1, bf16[3,3,3,384,384]{4,3,2,1,0:T(8,128)(2,1)} %wm_hbm.1, f32[384]{0:T(512)} %g2_ref.1, bf16[48,384]{1,0:T(8,128)(2,1)} %bitcast.6), custom_call_target="tpu_custom_call" | custom-call | tf_op jit(solution)/shard_map/pallas_call | solution.py:342
where the time goes:
time: 34.7 us; the launch traced here: 34.4 us
  Pallas kernels  34.2 us (99%)
    pallas_call x1, Pallas kernels, per_device(): pl.pallas_call(functools.partial(decode_kernel, (tiles, strips, hl, clat,...  23.3 us
    pallas_call x1, Pallas kernels, per_device(): pl.pallas_call(functools.partial(exchange_kernel, (tiles, strips, frames,...  10.9 us

commit v1 on v0

--- a/solution.py
+++ b/solution.py
@@ -29,17 +29,20 @@
     return jnp.where(rows == n - 1, 0.0, pltpu.roll(x, n - 1, 0))
 
 
-def exchange_kernel(sizes, lat_ref, got, pad_a, pad_b, packed, stage, send_sem, recv_sem, own_sem):
+def exchange_kernel(sizes, lat_hbm, got, lat_ref, pad_a, pad_b, packed, stage, send_sem, recv_sem, own_sem, lat_sem):
     tiles, strips, frames, shard_rows = sizes
     quarters = tiles // frames
     blocks = tiles // strips
     offset = strips // 2 - 1
     me = lax.axis_index("tile")
+    fetch = pltpu.make_async_copy(lat_hbm, lat_ref, lat_sem)
+    fetch.start()
     barrier = pltpu.get_barrier_semaphore()
     for step in range(1, tiles):
         pl.semaphore_signal(barrier, inc=1, device_id={"tile": lax.rem(me + step, tiles)})
 
     wl = lat_ref.shape[1]
+    fetch.wait()
     values = lat_ref[...].astype(jnp.float32)
     spare = jnp.zeros((2 * LANES - values.shape[0], wl), jnp.float32)
     for pad, rows in ((pad_a, values[:LANES]), (pad_b, jnp.concatenate([values[LANES:], spare]))):
@@ -325,15 +328,17 @@
     got = pl.pallas_call(
         functools.partial(exchange_kernel, (tiles, strips, frames, shard_rows)),
         out_shape=jax.ShapeDtypeStruct((slots, WIDE + HALF, LANES), jnp.bfloat16),
-        in_specs=[pl.BlockSpec(memory_space=pltpu.VMEM)],
+        in_specs=[pl.BlockSpec(memory_space=pl.ANY)],
         out_specs=pl.BlockSpec(memory_space=pl.ANY),
         scratch_shapes=[
+            pltpu.VMEM((shard_rows * clat, wl), jnp.bfloat16),
             pltpu.VMEM((8 + wl + WS, LANES), jnp.float32),
             pltpu.VMEM((8 + wl + WS, LANES), jnp.float32),
             pltpu.VMEM((strips, WIDE + HALF, LANES), jnp.float32),
             pltpu.VMEM((strips, WIDE + HALF, LANES), jnp.bfloat16),
             pltpu.SemaphoreType.DMA((3 * strips,)),
             pltpu.SemaphoreType.DMA((slots,)),
+            pltpu.SemaphoreType.DMA,
             pltpu.SemaphoreType.DMA,
         ],
         compiler_params=pltpu.CompilerParams(collective_id=0, has_side_effects=True),

time: 34.7 us -> 34.2 us (0.986)
  Pallas kernels: 34.2 us -> 33.8 us
    pallas_call x1, Pallas kernels: 10.9 us -> 10.2 us  [per_device(): pl.pallas_call(functools.partial(exchange_kernel, (tiles, strips, frames,...]
where the time goes in v1:
time: 34.2 us; the launch traced here: 34 us
  Pallas kernels  33.8 us (99%)
    pallas_call x1, Pallas kernels, per_device(): pl.pallas_call(functools.partial(decode_kernel, (tiles, strips, hl, clat,...  23.7 us
    pallas_call x1, Pallas kernels, per_device(): pl.pallas_call(functools.partial(exchange_kernel, (tiles, strips, frames,...  10.2 us

profile of v1, /device:TPU:0, one launch (start us, length us, event | category | flops | bytes accessed | tf_op | source)
XLA Modules:
  0.0 34.0 jit_solution(8910895252366511898)
XLA Ops:
  0.0 10.2 %shard_map.73.got_ref = bf16[24,32,128]{2,1,0:T(8,128)(2,1)} custom-call(bf16[192,128]{1,0:T(8,128)(2,1)} %bitcast.5), custom_call_target="tpu_custom_call" | custom-call | tf_op jit(solution)/shard_map/pallas_call | solution.py:328
  10.2 23.7 %shard_map.74 = f32[2,3,48,128]{3,2,1,0:T(8,128)} custom-call(s32[4]{0:T(128)} %clip.1, bf16[24,32,128]{2,1,0:T(8,128)(2,1)} %shard_map.73.got_ref, bf16[3,144,384]{2,1,0:T(8,128)(2,1)} %bitcast.4, f32[384]{0:T(512)} %g1_ref.1, bf16[3,3,3,384,384]{4,3,2,1,0:T(8,128)(2,1)} %wm_hbm.1, f32[384]{0:T(512)} %g2_ref.1, bf16[48,384]{1,0:T(8,128)(2,1)} %bitcast.6), custom_call_target="tpu_custom_call" | custom-call | tf_op jit(solution)/shard_map/pallas_call | solution.py:347
